TPU v7x, 32 devices: a whole 2x2x4 slice. The times are simulated.
32 devices in a mesh: dp: 8 (over y, x, core), vocab: 4 (over z).
Axes of the slice: x: 2, y: 2, z: 4, core: 2. Of those that a mesh axis runs over, the one named last changes fastest.
Arguments:
- student_hidden: bfloat16 [1024, 1536], P('dp'), may hold values from -16 to 16
- head_weight: bfloat16 [1536, 16384], P('dp', 'vocab'), may hold values from -1 to 1
- teacher_logprobs: float32 [1024, 20480], P('dp', 'vocab'), may hold values from -45 to 0, as said below
- align_index: int32 [128, 2], replicated, may hold values from 0 to 159, as said below
- align_tiles: bfloat16 [128, 2, 128, 128], P('vocab'), may hold values from 0 to 6.1
- grad_scale: float32 [1024], P('dp'), may hold values from 30 to 300
Outputs:
- hidden_grad: bfloat16 [1024, 1536], P('dp', 'vocab')
- head_grad: bfloat16 [1536, 16384], P('dp', 'vocab')
Inputs may be any that keep to these rules, and one draw needn't show every extreme that they name: `teacher_logprobs`: each row's exponentials sum to 1 over the 20480 teacher entries. `align_index`: teacher block j is held by vocab index j // 40. Of the 64 entries of the student blocks held by one vocab index, at most 32 name teacher blocks held by any one vocab index, and for every vocab index some vocab index holds exactly 32 of them.
All inputs are finite; a program needn't handle non-finite values.
Results may differ from a plain program's by a relative error of at most 0.015.
Values may be sent and summed in bfloat16 or wider, within the bound.
No kernel may reach another device: no remote copies, remote signals or barrier semaphores. Data moves between devices by JAX's collectives and lax.ppermute only.
A program may use at most 128 MiB of HBM per device.

v0:
```python
import jax
import jax.numpy as jnp
from jax import lax
from jax.sharding import PartitionSpec as P

BLOCK = 128
K = 2


def pair_tables(index_rows, teacher_count, vocab_count):
    owner_of = index_rows // teacher_count
    local_block = index_rows % teacher_count
    onehot = (owner_of[..., None] == jnp.arange(vocab_count)[None, None, :]).astype(jnp.int32)
    running = jnp.cumsum(onehot, axis=1)
    slot_rank = jnp.sum(onehot * running, axis=2) - 1
    return (owner_of, local_block, slot_rank)


def body(student_hidden, head_weight, teacher_logprobs, align_index, align_tiles, grad_scale):
    vocab_count = lax.axis_size("vocab")
    own_index = lax.axis_index("vocab")
    tokens_here = student_hidden.shape[0]
    student_cols = head_weight.shape[1]
    student_count = student_cols // BLOCK
    teacher_count = teacher_logprobs.shape[1] // BLOCK
    pair_count = student_count * K
    capacity = (2 * pair_count + vocab_count - 1) // vocab_count
    all_rows = align_index.reshape(vocab_count, pair_count)
    owner_all, local_all, rank_all = pair_tables(all_rows, teacher_count, vocab_count)
    held_here = owner_all == own_index
    slot_numbers = jnp.arange(capacity)
    selected = (
        held_here[:, None, :] & (rank_all[:, None, :] == slot_numbers[None, :, None])
    ).astype(jnp.int32)
    source_block = jnp.sum(selected * local_all[:, None, :], axis=2).reshape(-1)
    filled = jnp.sum(selected, axis=2).reshape(-1) > 0
    teacher_probs = (
        jnp.exp(teacher_logprobs).astype(jnp.bfloat16).reshape(tokens_here, teacher_count, BLOCK)
    )
    outgoing = jnp.take(teacher_probs, source_block, axis=1)
    outgoing = jnp.where(filled[None, :, None], outgoing, jnp.zeros_like(outgoing))
    own_owner = lax.dynamic_index_in_dim(owner_all, own_index, 0, keepdims=False)
    own_rank = lax.dynamic_index_in_dim(rank_all, own_index, 0, keepdims=False)
    where_from = own_owner * capacity + own_rank
    arrived = lax.all_to_all(outgoing, "vocab", split_axis=1, concat_axis=1, tiled=True)
    picked = jnp.take(arrived, where_from, axis=1).reshape(
        arrived.shape[0], student_count, K, BLOCK
    )
    mapped_rows = jnp.einsum(
        "tbkj,bkji->tbi", picked, align_tiles, preferred_element_type=jnp.float32
    )
    mapped = mapped_rows.reshape(arrived.shape[0], student_cols)
    piece = lax.all_gather(head_weight, "dp", axis=0, tiled=True)
    feature_cols = student_hidden
    partial_logits = jnp.dot(feature_cols, piece, preferred_element_type=jnp.float32)
    row_max = lax.pmax(jnp.max(partial_logits, axis=1), "vocab")
    shifted = jnp.exp(partial_logits - row_max[:, None])
    row_total, mass = lax.psum((jnp.sum(shifted, axis=1), jnp.sum(mapped, axis=1)), "vocab")
    student_probs = shifted / row_total[:, None]
    dlogits = (grad_scale[:, None] * (mass[:, None] * student_probs - mapped)).astype(jnp.bfloat16)
    hidden_terms = lax.dot_general(
        dlogits, piece, (((1,), (1,)), ((), ())), preferred_element_type=jnp.float32
    )
    hidden_grad = lax.psum_scatter(
        hidden_terms.astype(jnp.bfloat16), "vocab", scatter_dimension=1, tiled=True
    )
    feature_cols = student_hidden
    head_grad = lax.psum_scatter(
        lax.dot_general(
            feature_cols, dlogits, (((0,), (0,)), ((), ())), preferred_element_type=jnp.float32
        ).astype(jnp.bfloat16),
        "dp",
        scatter_dimension=0,
        tiled=True,
    )
    return (hidden_grad, head_grad)


def solution(mesh):
    placed = (
        P("dp", None),
        P("dp", "vocab"),
        P("dp", "vocab"),
        P(),
        P("vocab", None, None, None),
        P("dp"),
    )
    return jax.shard_map(
        body,
        mesh=mesh,
        in_specs=placed,
        out_specs=(P("dp", "vocab"), P("dp", "vocab")),
        check_vma=False,
    )
```

profile of v0, /device:TPU:0, one launch (start us, length us, event | category | flops | bytes accessed | tf_op | source)
XLA Modules:
  0.0 297.2 jit_solution(14028854134942604966)
XLA Ops:
  7.2 0.0 copy-start
  7.2 0.0 all-gather.2.cloned.1.call-start
  7.2 0.7 all-gather.2.cloned.1.call-update
  7.9 0.7 sign_compare_fusion
  8.6 0.1 copy.34
  8.7 0.1 ne.50
  8.9 0.7 broadcast_remainder_fusion
  9.6 0.1 copy.35
  9.7 0.1 rem.30
  9.8 0.1 copy.36
  9.9 0.1 div.26
  10.0 0.1 fusion.6
  10.1 0.1 reduce_window_sum.11
  10.3 0.2 select_reduce_fusion
  10.5 0.2 convert_reduce_fusion
  10.7 0.1 reshape.166
  10.8 0.1 reshape.164
  10.9 0.1 gt.19
  11.0 3.2 %copy.37 = f32[128,5120]{0,1:T(8,128)} copy(f32[128,5120]{1,0:T(8,128)} %param.8) | data formatting | bytes 5242880 | tf_op args[2]
  14.2 3.1 %exponential_convert_fusion = bf16[128,5120]{0,1:T(8,128)(2,1)} fusion(f32[128,5120]{0,1:T(8,128)} %copy.37), kind=kLoop, calls=%fused_computation.5 | loop fusion | flops 655360 | bytes 3932160 | tf_op jit(solution)/shard_map/convert_element_type | solution.py:38
  17.4 1.8 copy.38
  19.1 3.0 %gather_fusion = bf16[128,128,128]{2,1,0:T(8,128)(2,1)} fusion(bf16[128,40,128]{2,0,1:T(8,128)(2,1)S(1)} %copy.38, s32[1024]{0:T(1024)S(1)} %pad_clamp_fusion.1), kind=kCustom, calls=%fused_computation | custom fusion | bytes 8389120 | tf_op jit(solution)/shard_map/jit(_take)/gather | solution.py:40
  22.2 4.4 %select_bitcast_fusion = bf16[128,128,128]{2,0,1:T(8,128)(2,1)} fusion(bf16[128,128,128]{2,1,0:T(8,128)(2,1)} %gather_fusion, pred[128]{0:T(512)(128)(4,1)S(1)} %gt.19, pred[128]{0:T(512)(128)(4,1)S(1)} %compare_and_fusion.1), kind=kLoop, calls=%fused_computation.4 | loop fusion | flops 4194304 | bytes 8388864 | tf_op jit(solution)/shard_map/jit(_where)/select_n | solution.py:41
  26.6 6.1 %all-to-all-start = ((bf16[128,128,128]{2,0,1:T(8,128)(2,1)}), bf16[128,128,128]{2,0,1:T(8,128)(2,1)}, u32[]{:S(2)}, u32[]{:S(2)}) async-start(bf16[128,128,128]{2,0,1:T(8,128)(2,1)} %select_bitcast_fusion), calls=%async_computation | async-start | bytes 8388608 | tf_op jit(solution)/shard_map/all_to_all | solution.py:45
  32.7 0.0 reduce-scatter.7.cloned.1.call-start
  32.7 0.5 broadcast.185
  33.2 0.7 fusion.11
  33.9 0.1 add.101
  34.0 92.1 %all-to-all-done = bf16[128,128,128]{2,0,1:T(8,128)(2,1)} async-done(((bf16[128,128,128]{2,0,1:T(8,128)(2,1)}), bf16[128,128,128]{2,0,1:T(8,128)(2,1)}, u32[]{:S(2)}, u32[]{:S(2)}) %all-to-all-start) | async-done | bytes 4194336 | tf_op jit(solution)/shard_map/all_to_all | solution.py:45
  126.1 4.4 %gather_fusion.1 = bf16[64,128,128]{2,1,0:T(8,128)(2,1)} fusion(bf16[128,128,128]{2,0,1:T(8,128)(2,1)} %all-to-all-done, s32[1024]{0:T(1024)S(1)} %pad_clamp_fusion), kind=kCustom, calls=%fused_computation.1 | custom fusion | bytes 4194560 | tf_op jit(solution)/shard_map/jit(_take)/gather | solution.py:46
  130.5 0.0 copy-done
  130.5 3.8 %bitcast_reduce_fusion = (f32[128]{0:T(128)S(1)}, f32[32,128,128,1]{1,2,3,0:T(8,128)}) fusion(bf16[32,2,128,128]{3,2,1,0:T(8,128)(2,1)S(1)} %copy-done, bf16[128,32,2,128]{3,0,2,1:T(8,128)(2,1)} %bitcast.29, pred[32,2]{1,0:T(8,128)(4,1)S(1)} %compare_and_fusion), kind=kOutput, calls=%fused_computation.7 | convolution fusion | flops 270008192 | bytes 6292032 | tf_op jit(solution)/shard_map/tbkj,bkji->tbi/dot_general | solution.py:49
  134.3 0.0 copy-start.2
  134.3 3.0 %copy.40 = f32[128,4096]{1,0:T(8,128)} copy(f32[128,4096]{0,1:T(8,128)} %bitcast.30) | data formatting | bytes 4194304 | tf_op jit(solution)/shard_map/reshape | solution.py:52
  137.2 0.0 all-gather.2.cloned.1.call-done
  137.2 0.0 copy-done.2
  137.2 6.5 %fusion.12 = (f32[128]{0:T(128)S(1)}, f32[128,4096]{1,0:T(8,128)S(1)}) fusion(bf16[128,1536]{1,0:T(8,128)(2,1)S(1)} %copy-done.2, bf16[1536,4096]{1,0:T(8,128)(2,1)} %all-gather.2.cloned.1.call-done), kind=kOutput, calls=%fused_computation.44 | convolution fusion | flops 1611136896 | bytes 15073792 | tf_op jit(solution)/shard_map/dot_general | solution.py:55
  143.7 0.0 copy-start.3
  143.7 9.8 %pmax.7 = f32[128]{0:T(128)S(1)} all-reduce(f32[128]{0:T(128)S(1)} %get-tuple-element.22), channel_id=1, replica_groups=mesh['dp'=8,'vocab'=4] {'vocab'}, use_global_device_ids=true, to_apply=%region_7.8 | all-reduce | flops 128 | bytes 1024 | tf_op jit(solution)/shard_map/pmax | solution.py:56
  153.5 0.4 fusion.4
  153.9 9.1 %all-reduce = (f32[128]{0:T(128)S(1)}, f32[128]{0:T(128)S(1)}) all-reduce(f32[128]{0:T(128)S(1)} %fusion.4, f32[128]{0:T(128)S(1)} %get-tuple-element.24), channel_id=1, replica_groups=mesh['dp'=8,'vocab'=4] {'vocab'}, use_global_device_ids=true, to_apply=%region_9.10 | all-reduce | flops 256 | bytes 2048 | tf_op jit(solution)/shard_map/psum | solution.py:58
  163.0 0.0 copy-done.3
  163.0 9.5 %convolution_convert_fusion.1 = bf16[128,1536]{1,0:T(8,128)(2,1)S(1)} fusion(bf16[1536,4096]{1,0:T(8,128)(2,1)} %all-gather.2.cloned.1.call-done, f32[128,4096]{1,0:T(8,128)} %copy.40, f32[128,4096]{1,0:T(8,128)S(1)} %get-tuple-element.23, f32[128]{0:T(128)S(1)} %get-tuple-element.14, f32[128]{0:T(128)S(1)} %pmax.7, f32[128]{0:T(128)S(1)} %get-tuple-element.15, ...), kind=kOutput, calls=%fused_computation.6 | convolution fusion | flops 1613955072 | bytes 17172480 | tf_op jit(solution)/shard_map/dot_general | solution.py:61
  172.5 0.9 copy.44
  173.4 0.0 reduce-scatter.7.cloned.1.call-update
  173.4 0.2 reduce-scatter.9.cloned.1.call-start
  173.7 8.8 %fusion = bf16[1536,4096]{0,1:T(8,128)(2,1)} fusion(bf16[128,1536]{1,0:T(8,128)(2,1)S(1)} %copy-done.2, f32[128,4096]{1,0:T(8,128)} %copy.40, f32[128,4096]{1,0:T(8,128)S(1)} %get-tuple-element.23, f32[128]{0:T(128)S(1)} %get-tuple-element.14, f32[128]{0:T(128)S(1)} %pmax.7, f32[128]{0:T(128)S(1)} %get-tuple-element.15, f32[128]{0:T(128)S(1)} %copy-done.3), kind=kOutput, calls=%fused_computation.3 | convolution fusion | flops 1620049920 | bytes 17172480 | tf_op jit(solution)/shard_map/dot_general | solution.py:69
  182.5 16.7 %copy.46 = bf16[1536,4096]{1,0:T(8,128)(2,1)} copy(bf16[1536,4096]{0,1:T(8,128)(2,1)} %fusion) | data formatting | bytes 25165824
  199.1 0.0 reduce-scatter.9.cloned.1.call-update
  199.1 0.0 copy-start.1
  199.2 0.0 reduce-scatter.7.cloned.1.call-done
  199.2 1.8 copy.45
  201.0 89.7 %reduce-scatter.9.cloned.1.call-done = bf16[192,4096]{1,0:T(8,128)(2,1)} async-done(((bf16[1536,4096]{1,0:T(8,128)(2,1)}), bf16[192,4096]{1,0:T(8,128)(2,1)}) %reduce-scatter.9.cloned.1.call-update) | async-done | bytes 1572880
  290.6 0.0 copy-done.1
  (9 shorter events, 0.1 us)
Async XLA Ops:
  7.2 123.3 %copy-start = (bf16[32,2,128,128]{3,2,1,0:T(8,128)(2,1)S(1)}, bf16[32,2,128,128]{3,2,1,0:T(8,128)(2,1)}, u32[]{:S(2)}) copy-start(bf16[32,2,128,128]{3,2,1,0:T(8,128)(2,1)} %param.10) | copy-start | bytes 6291460
  7.2 130.1 %all-gather.2.cloned.1.call-start = ((), (), s32[]{:S(2)}) async-start(), calls=%async_computation.3 | async-start | bytes 14155776 | tf_op jit(solution)/shard_map/all_gather | solution.py:53
  26.6 99.5 %all-to-all-start = ((bf16[128,128,128]{2,0,1:T(8,128)(2,1)}), bf16[128,128,128]{2,0,1:T(8,128)(2,1)}, u32[]{:S(2)}, u32[]{:S(2)}) async-start(bf16[128,128,128]{2,0,1:T(8,128)(2,1)} %select_bitcast_fusion), calls=%async_computation | async-start | bytes 8388608 | tf_op jit(solution)/shard_map/all_to_all | solution.py:45
  32.7 166.5 %reduce-scatter.7.cloned.1.call-start = ((), (), s32[]{:S(2)}) async-start(), calls=%async_computation.4 | async-start | bytes 491520
  134.3 3.0 %copy-start.2 = (bf16[128,1536]{1,0:T(8,128)(2,1)S(1)}, bf16[128,1536]{1,0:T(8,128)(2,1)}, u32[]{:S(2)}) copy-start(bf16[128,1536]{1,0:T(8,128)(2,1)} %param.6) | copy-start | bytes 1179652
  143.7 19.3 %copy-start.3 = (f32[128]{0:T(128)S(1)}, f32[128]{0:T(128)}, u32[]{:S(2)}) copy-start(f32[128]{0:T(128)} %param.11) | copy-start | bytes 1540
  173.4 117.2 %reduce-scatter.9.cloned.1.call-start = ((), (), s32[]{:S(2)}) async-start(), calls=%async_computation.5 | async-start | bytes 14155776
  199.1 91.5 %copy-start.1 = (bf16[32,2,128,128]{3,2,1,0:T(8,128)(2,1)S(1)}, bf16[32,2,128,128]{3,2,1,0:T(8,128)(2,1)}, u32[]{:S(2)}) copy-start(bf16[32,2,128,128]{3,2,1,0:T(8,128)(2,1)} %param.10) | copy-start | bytes 6291460
Sparse Core Ops, SparseCore 0:
  9.9 74.7 all-gather.1
  173.6 19.8 reduce-scatter.6
  199.3 91.3 reduce-scatter.8
where the time goes:
time: 298 us; the launch traced here: 297 us
  waiting for transfers between devices  183 us (61%)
  local copies, waits for them, and re-layouts  36.3 us (12%)
  matrix products  28.5 us (10%)
  blocking collectives  18.8 us (6%)
  between operations  13.9 us (5%)
  other arithmetic  10.8 us (4%)
  starting transfers between devices  6.36 us (2%)
    all_to_all x1, waiting for transfers between devices, body(): lax.all_to_all(outgoing, 'vocab', split_axis=1, concat_axis=1, tiled=True)  92.1 us
    unnamed x5, waiting for transfers between devices  90.4 us
    unnamed x12, local copies, waits for them, and re-layouts  22.6 us
    pmax x1, blocking collectives, body(): row_max = lax.pmax(jnp.max(partial_logits, axis=1), 'vocab')  9.76 us
    dot_general x1, matrix products, body(): lax.dot_general(dlogits, piece, (((1,), (1,)), ((), ())), preferred_eleme...  9.49 us
    psum x1, blocking collectives, body(): lax.psum((jnp.sum(shifted, axis=1), jnp.sum(mapped, axis=1)), 'vocab')  9.08 us
    dot_general x1, matrix products, body(): lax.dot_general(feature_cols, dlogits, (((0,), (0,)), ((), ())), preferre...  8.81 us
    dot_general x1, matrix products, body(): jnp.dot(feature_cols, piece, preferred_element_type=jnp.float32)  6.46 us
  transfers between devices with their start and end apart: 4, of which 2 were waited for; matrix products, arithmetic and copies ran while one was open for 20% of the time, Pallas kernels for 0%

commit v1 on v0

v1 whole, which is shorter than its diff:
```python
import jax
import jax.numpy as jnp
from jax import lax
from jax.sharding import PartitionSpec as P

BLOCK = 128
K = 2


def pair_tables(index_rows, teacher_count, vocab_count):
    owner_of = index_rows // teacher_count
    local_block = index_rows % teacher_count
    onehot = (owner_of[..., None] == jnp.arange(vocab_count)[None, None, :]).astype(jnp.int32)
    running = jnp.cumsum(onehot, axis=1)
    slot_rank = jnp.sum(onehot * running, axis=2) - 1
    return (owner_of, local_block, slot_rank)


def gather_rows(x, axis):
    count = lax.axis_size(axis)
    copies = jnp.broadcast_to(x[None], (count,) + x.shape).reshape((count * x.shape[0],) + x.shape[1:])
    return lax.all_to_all(copies, axis, split_axis=0, concat_axis=0, tiled=True)


def scatter_hidden(partial):
    dp = lax.axis_size("dp")
    vocab = lax.axis_size("vocab")
    core = lax.axis_index("dp") % 2
    tokens, features = partial.shape[0] // dp, partial.shape[1]
    parts = partial.astype(jnp.bfloat16).reshape(dp // 2, 2, tokens, features)
    kept = lax.dynamic_index_in_dim(parts, core, 1, keepdims=False)
    sent = lax.dynamic_index_in_dim(parts, 1 - core, 1, keepdims=False)
    got = lax.ppermute(sent, "dp", [(i, i ^ 1) for i in range(dp)])
    both = (kept.astype(jnp.float32) + got.astype(jnp.float32)).astype(jnp.bfloat16)
    groups = [[i for i in range(dp) if i % 2 == c] for c in range(2)]
    rows = lax.all_to_all(both, "dp", split_axis=0, concat_axis=0, axis_index_groups=groups, tiled=True)
    rows = jnp.sum(rows.astype(jnp.float32), axis=0).astype(jnp.bfloat16)
    last = rows.reshape(tokens, vocab, features // vocab).transpose(1, 0, 2)
    last = lax.all_to_all(last, "vocab", split_axis=0, concat_axis=0, tiled=True)
    return jnp.sum(last.astype(jnp.float32), axis=0).astype(jnp.bfloat16)


def body(student_hidden, head_weight, teacher_logprobs, align_index, align_tiles, grad_scale):
    vocab_count = lax.axis_size("vocab")
    dp_count = lax.axis_size("dp")
    own_index = lax.axis_index("vocab")
    dp_index = lax.axis_index("dp")
    tokens_here = student_hidden.shape[0]
    student_cols = head_weight.shape[1]
    student_count = student_cols // BLOCK
    teacher_count = teacher_logprobs.shape[1] // BLOCK
    pair_count = student_count * K
    capacity = (2 * pair_count + vocab_count - 1) // vocab_count
    all_rows = align_index.reshape(vocab_count, pair_count)
    owner_all, local_all, rank_all = pair_tables(all_rows, teacher_count, vocab_count)
    held_here = owner_all == own_index
    slot_numbers = jnp.arange(capacity)
    selected = (
        held_here[:, None, :] & (rank_all[:, None, :] == slot_numbers[None, :, None])
    ).astype(jnp.int32)
    source_block = jnp.sum(selected * local_all[:, None, :], axis=2).reshape(-1)
    own_owner = lax.dynamic_index_in_dim(owner_all, own_index, 0, keepdims=False)
    own_rank = lax.dynamic_index_in_dim(rank_all, own_index, 0, keepdims=False)
    where_from = own_owner * capacity + own_rank

    teacher_probs = (
        jnp.exp(teacher_logprobs).astype(jnp.bfloat16).reshape(tokens_here, teacher_count, BLOCK)
    ).transpose(1, 0, 2)
    outgoing = jnp.take(teacher_probs, source_block, axis=0)
    arrived = lax.all_to_all(outgoing, "vocab", split_axis=0, concat_axis=0, tiled=True)

    weight = lax.all_to_all(head_weight, "dp", split_axis=1, concat_axis=0, tiled=True)
    hidden = gather_rows(student_hidden, "dp")
    logits = jnp.dot(hidden, weight, preferred_element_type=jnp.float32)
    row_max = lax.pmax(jnp.max(logits, axis=1), ("dp", "vocab"))
    shifted = jnp.exp(logits - row_max[:, None])

    picked = jnp.take(arrived, where_from, axis=0).reshape(student_count, K, tokens_here, BLOCK)
    mapped_rows = jnp.einsum("bktj,bkji->tbi", picked, align_tiles, preferred_element_type=jnp.float32)
    mapped_rows = mapped_rows.reshape(tokens_here, student_cols)
    mapped = lax.all_to_all(
        mapped_rows.astype(jnp.bfloat16), "dp", split_axis=1, concat_axis=0, tiled=True
    )
    own_rows = (jnp.arange(dp_count) == dp_index).astype(jnp.float32)[:, None]
    first = (own_index == 0).astype(jnp.float32)
    mass_part = (own_rows * jnp.sum(mapped_rows, axis=1)[None]).reshape(-1)
    scale_part = (own_rows * (first * grad_scale)[None]).reshape(-1)
    row_total, mass, scale = lax.psum((jnp.sum(shifted, axis=1), mass_part, scale_part), ("dp", "vocab"))
    student_probs = shifted / row_total[:, None]
    dlogits = (
        scale[:, None] * (mass[:, None] * student_probs - mapped.astype(jnp.float32))
    ).astype(jnp.bfloat16)
    hidden_terms = lax.dot_general(
        dlogits, weight, (((1,), (1,)), ((), ())), preferred_element_type=jnp.float32
    )
    hidden_grad = scatter_hidden(hidden_terms)
    head_terms = lax.dot_general(
        hidden, dlogits, (((0,), (0,)), ((), ())), preferred_element_type=jnp.float32
    ).astype(jnp.bfloat16)
    head_grad = lax.all_to_all(head_terms, "dp", split_axis=0, concat_axis=1, tiled=True)
    return (hidden_grad, head_grad)


def solution(mesh):
    placed = (
        P("dp", None),
        P("dp", "vocab"),
        P("dp", "vocab"),
        P(),
        P("vocab", None, None, None),
        P("dp"),
    )
    return jax.shard_map(
        body,
        mesh=mesh,
        in_specs=placed,
        out_specs=(P("dp", "vocab"), P("dp", "vocab")),
        check_vma=False,
    )
```

time: 298 us -> 345 us (1.16)
  blocking collectives: 18.8 us -> 177 us
  waiting for transfers between devices: 183 us -> 72.9 us
  starting transfers between devices: 6.36 us -> 26.1 us
  between operations: 13.9 us -> 0.88 us
  matrix products: 28.5 us -> 18.2 us
  other arithmetic: 10.8 us -> 19.8 us
  local copies, waits for them, and re-layouts: 36.3 us -> 28.3 us
    all_to_all x0 -> x1, blocking collectives: none -> 96.8 us  [body(): lax.all_to_all(outgoing, 'vocab', split_axis=0, concat_axis=0, tiled=True)]
    unnamed x5 -> x0, waiting for transfers between devices: 90.4 us -> none
    pmax x1, blocking collectives: 9.76 us -> 41.2 us  [body(): row_max = lax.pmax(jnp.max(logits, axis=1), ('dp', 'vocab'))]
    psum x1, blocking collectives: 9.08 us -> 39.5 us  [body(): lax.psum((jnp.sum(shifted, axis=1), mass_part, scale_part), ('dp', 'vocab'))]
    all_to_all x1 -> x6, waiting for transfers between devices: 92.1 us -> 69.2 us  [the longest x1 28.2 us: gather_rows(): return lax.all_to_all(copies, axis, split_axis=0, concat_axis=0, tiled=True)]
    all_to_all x1 -> x6, starting transfers between devices: 6.1 us -> 26.1 us  [the longest x1 5.33 us: body(): lax.all_to_all(head_weight, 'dp', split_axis=1, concat_axis=0, tiled=True)]
    unnamed x12 -> x17, local copies, waits for them, and re-layouts: 22.6 us -> 5.08 us
    dot_general x4, matrix products: 28.5 us -> 18.2 us  [the longest x1 5.49 us: body(): logits = jnp.dot(hidden, weight, preferred_element_type=jnp.float32)]
  transfers between devices with their start and end apart: 4 -> 7, of which waited for: 2 -> 6; matrix products, arithmetic and copies ran while one was open for 20% -> 14% of each run, Pallas kernels for 0% -> 0%
where the time goes in v1:
time: 345 us; the launch traced here: 343 us
  blocking collectives  177 us (51%)
  waiting for transfers between devices  72.9 us (21%)
  local copies, waits for them, and re-layouts  28.3 us (8%)
  starting transfers between devices  26.1 us (8%)
  other arithmetic  19.8 us (6%)
  matrix products  18.2 us (5%)
    all_to_all x1, blocking collectives, body(): lax.all_to_all(outgoing, 'vocab', split_axis=0, concat_axis=0, tiled=True)  96.8 us
    pmax x1, blocking collectives, body(): row_max = lax.pmax(jnp.max(logits, axis=1), ('dp', 'vocab'))  41.2 us
    psum x1, blocking collectives, body(): lax.psum((jnp.sum(shifted, axis=1), mass_part, scale_part), ('dp', 'vocab'))  39.5 us
    all_to_all x1, waiting for transfers between devices, gather_rows(): return lax.all_to_all(copies, axis, split_axis=0, concat_axis=0, tiled=True)  28.2 us
    all_to_all x1, waiting for transfers between devices, body(): lax.all_to_all(head_terms, 'dp', split_axis=0, concat_axis=1, tiled=True)  18.2 us
    all_to_all x1, waiting for transfers between devices, scatter_hidden(): lax.all_to_all(both, 'dp', split_axis=0, concat_axis=0, axis_index_groups...  12.9 us
  transfers between devices with their start and end apart: 7, of which 6 were waited for; matrix products, arithmetic and copies ran while one was open for 14% of the time, Pallas kernels for 0%

profile of v1, /device:TPU:0, one launch (start us, length us, event | category | flops | bytes accessed | tf_op | source)
XLA Modules:
  0.0 343.5 jit_solution(2397335683305660772)
XLA Ops:
  0.6 0.0 copy-start
  0.6 2.8 copy.83
  3.5 5.3 %all-to-all-start.2 = ((bf16[192,8,512]{2,0,1:T(8,128)(2,1)}), bf16[192,8,512]{2,0,1:T(8,128)(2,1)}, u32[]{:S(2)}, u32[]{:S(2)}) async-start(bf16[192,8,512]{2,0,1:T(8,128)(2,1)} %bitcast.64), calls=%async_computation.2 | async-start | bytes 3145728 | tf_op jit(solution)/shard_map/all_to_all | solution.py:72
  8.8 0.0 copy-done.6
  8.9 0.1 copy.62
  9.0 0.1 ne.56
  9.1 0.1 copy.64
  9.2 0.1 div.26
  9.3 0.1 copy.63
  9.5 0.1 rem.44
  9.6 0.1 fusion.9
  9.7 3.2 copy.65
  12.9 3.2 exponential_convert_fusion
  16.1 0.1 reduce_window_sum.11
  16.2 0.2 select_reduce_fusion
  16.5 0.1 select_reduce_fusion.1
  16.6 0.1 reshape.197
  16.7 0.1 reshape.195
  16.8 1.8 copy.66
  18.6 3.1 gather_fusion
  21.7 4.6 %broadcast_select_fusion = bf16[128,128,128]{2,1,0:T(8,128)(2,1)} fusion(bf16[128,128,128]{2,1,0:T(8,128)(2,1)} %gather_fusion, pred[128]{0:T(512)(128)(4,1)S(1)} %compare_and_fusion.1), kind=kLoop, calls=%fused_computation.2 | loop fusion | flops 2097152 | bytes 8388736 | tf_op jit(solution)/shard_map/jit(_take)/select_n | solution.py:69
  26.3 3.7 %all-to-all-done.2 = bf16[192,8,512]{2,0,1:T(8,128)(2,1)} async-done(((bf16[192,8,512]{2,0,1:T(8,128)(2,1)}), bf16[192,8,512]{2,0,1:T(8,128)(2,1)}, u32[]{:S(2)}, u32[]{:S(2)}) %all-to-all-start.2) | async-done | bytes 1572896 | tf_op jit(solution)/shard_map/all_to_all | solution.py:72
  29.9 96.8 %all_to_all.72 = bf16[128,128,128]{2,1,0:T(8,128)(2,1)} all-to-all(bf16[128,128,128]{2,1,0:T(8,128)(2,1)} %broadcast_select_fusion), channel_id=1, replica_groups=mesh['dp'=8,'vocab'=4] {'vocab'}, dimensions={0} | all-to-all | bytes 8388608 | tf_op jit(solution)/shard_map/all_to_all | solution.py:70
  126.7 0.0 copy-done.5
  126.7 2.0 broadcast_in_dim.26
  128.7 4.9 %all-to-all-start.1 = ((bf16[8,128,1536]{2,1,0:T(8,128)(2,1)}), bf16[8,128,1536]{2,1,0:T(8,128)(2,1)}, u32[]{:S(2)}, u32[]{:S(2)}) async-start(bf16[8,128,1536]{2,1,0:T(8,128)(2,1)} %broadcast_in_dim.26), calls=%async_computation.1 | async-start | bytes 6291456 | tf_op jit(solution)/shard_map/all_to_all | solution.py:22
  133.6 0.5 broadcast.181
  134.1 0.7 fusion.16
  134.8 0.1 add.114
  135.0 0.0 copy-done.7
  135.0 4.3 %gather_fusion.1 = bf16[64,128,128]{2,1,0:T(8,128)(2,1)} fusion(bf16[128,128,128]{2,1,0:T(8,128)(2,1)} %all_to_all.72, s32[1024]{0:T(1024)S(1)} %pad_clamp_fusion), kind=kCustom, calls=%fused_computation.1 | custom fusion | bytes 4194560 | tf_op jit(solution)/shard_map/jit(_take)/gather | solution.py:78
  139.3 4.1 %bitcast_convert_fusion = (bf16[32,128,128]{1,2,0:T(8,128)(2,1)}, f32[32,128,128,1]{1,2,3,0:T(8,128)}) fusion(bf16[32,2,128,128]{3,2,1,0:T(8,128)(2,1)S(1)} %copy-done, bf16[32,2,128,128]{3,2,1,0:T(8,128)(2,1)} %bitcast.63, pred[32,2]{1,0:T(8,128)(4,1)S(1)} %compare_and_fusion), kind=kOutput, calls=%fused_computation.12 | convolution fusion | flops 270008320 | bytes 7340096 | tf_op jit(solution)/shard_map/bktj,bkji->tbi/dot_general | solution.py:79
  143.4 28.2 %all-to-all-done.1 = bf16[8,128,1536]{2,1,0:T(8,128)(2,1)} async-done(((bf16[8,128,1536]{2,1,0:T(8,128)(2,1)}), bf16[8,128,1536]{2,1,0:T(8,128)(2,1)}, u32[]{:S(2)}, u32[]{:S(2)}) %all-to-all-start.1) | async-done | bytes 3145760 | tf_op jit(solution)/shard_map/all_to_all | solution.py:22
  171.6 3.6 %all-to-all-start.3 = ((bf16[128,8,512]{0,2,1:T(8,128)(2,1)}), bf16[128,8,512]{0,2,1:T(8,128)(2,1)S(1)}, u32[]{:S(2)}, u32[]{:S(2)}) async-start(bf16[128,8,512]{0,2,1:T(8,128)(2,1)} %bitcast.14), calls=%async_computation.3 | async-start | bytes 2097152 | tf_op jit(solution)/shard_map/all_to_all | solution.py:81
  175.1 5.5 %fusion.18 = (f32[1024]{0:T(1024)S(1)}, f32[1024,512]{0,1:T(8,128)}) fusion(bf16[1024,1536]{1,0:T(8,128)(2,1)} %bitcast.10, bf16[1536,512]{1,0:T(8,128)(2,1)} %bitcast.12), kind=kOutput, calls=%fused_computation.57 | convolution fusion | flops 1611136000 | bytes 6819840 | tf_op jit(solution)/shard_map/dot_general | solution.py:74
  180.6 41.2 %pmax.7 = f32[1024]{0:T(1024)S(1)} all-reduce(f32[1024]{0:T(1024)S(1)} %get-tuple-element.15), channel_id=1, replica_groups=mesh['dp'=8,'vocab'=4] {'dp','vocab'}, use_global_device_ids=true, to_apply=%region_7.8 | all-reduce | flops 1024 | bytes 8192 | tf_op jit(solution)/shard_map/pmax | solution.py:75
  221.8 2.1 fusion.7
  223.8 0.2 copy-done.1
  224.0 0.6 bitcast_reduce_fusion
  224.6 0.1 multiply_bitcast_fusion.1
  224.6 39.5 %all-reduce = (f32[1024]{0:T(1024)S(1)}, f32[1024]{0:T(1024)S(1)}, f32[1024]{0:T(1024)S(1)}) all-reduce(f32[1024]{0:T(1024)S(1)} %fusion.7, f32[1024]{0:T(1024)S(1)} %get-tuple-element.12, f32[1024]{0:T(1024)S(1)} %get-tuple-element.11), channel_id=1, replica_groups=mesh['dp'=8,'vocab'=4] {'dp','vocab'}, use_global_device_ids=true, to_apply=%region_9.10 | all-reduce | flops 3072 | bytes 24576 | tf_op jit(solution)/shard_map/psum | solution.py:88
  264.1 0.0 all-to-all-done.3
  264.1 2.2 fusion.3
  266.3 3.6 %convolution_convert_fusion = bf16[1024,1536]{1,0:T(8,128)(2,1)S(1)} fusion(bf16[1024,512]{0,1:T(8,128)(2,1)S(1)} %fusion.3, bf16[1536,512]{1,0:T(8,128)(2,1)} %bitcast.12), kind=kOutput, calls=%fused_computation.3 | convolution fusion | flops 1612185600 | bytes 5767168 | tf_op jit(solution)/shard_map/dot_general | solution.py:93
  270.0 0.0 copy-done.3
  270.0 0.0 copy-start.2
  270.0 1.7 copy-done.2
  271.7 1.2 dynamic-slice_bitcast_fusion
  272.9 0.0 collective-permute-start
  272.9 3.7 %collective-permute-done = bf16[4,128,1536]{2,1,0:T(8,128)(2,1)} collective-permute-done((bf16[4,128,1536]{2,1,0:T(8,128)(2,1)}, bf16[4,128,1536]{2,1,0:T(8,128)(2,1)}, u32[]{:S(2)}, u32[]{:S(2)}) %collective-permute-start) | collective-permute-done | bytes 1572896 | tf_op jit(solution)/shard_map/ppermute | solution.py:33
  276.7 3.4 fusion
  280.1 4.5 %all-to-all-start.4 = ((bf16[4,128,1536]{2,1,0:T(8,128)(2,1)}), bf16[4,128,1536]{2,1,0:T(8,128)(2,1)}, u32[]{:S(2)}, u32[]{:S(2)}) async-start(bf16[4,128,1536]{2,1,0:T(8,128)(2,1)} %fusion), calls=%async_computation.4 | async-start | bytes 3145728 | tf_op jit(solution)/shard_map/all_to_all | solution.py:36
  284.6 4.9 %fusion.1 = bf16[1536,512]{0,1:T(8,128)(2,1)} fusion(bf16[1024,512]{0,1:T(8,128)(2,1)S(1)} %copy-done.4, bf16[1024,1536]{1,0:T(8,128)(2,1)} %bitcast.10), kind=kOutput, calls=%fused_computation.7 | convolution fusion | flops 1611399168 | bytes 5767168 | tf_op jit(solution)/shard_map/dot_general | solution.py:97
  289.5 2.6 copy.73
  292.1 12.9 %all-to-all-done.4 = bf16[4,128,1536]{2,1,0:T(8,128)(2,1)} async-done(((bf16[4,128,1536]{2,1,0:T(8,128)(2,1)}), bf16[4,128,1536]{2,1,0:T(8,128)(2,1)}, u32[]{:S(2)}, u32[]{:S(2)}) %all-to-all-start.4) | async-done | bytes 1572896 | tf_op jit(solution)/shard_map/all_to_all | solution.py:36
  305.0 4.3 %all-to-all-start.6 = ((bf16[8,192,512]{2,1,0:T(8,128)(2,1)}), bf16[8,192,512]{2,1,0:T(8,128)(2,1)}, u32[]{:S(2)}, u32[]{:S(2)}) async-start(bf16[8,192,512]{2,1,0:T(8,128)(2,1)} %bitcast.65), calls=%async_computation.6 | async-start | bytes 3145728 | tf_op jit(solution)/shard_map/all_to_all | solution.py:100
  309.3 1.7 reduce_sum.64
  311.0 0.2 copy.71
  311.2 0.9 copy.72
  312.1 18.2 %all-to-all-done.6 = bf16[8,192,512]{2,1,0:T(8,128)(2,1)} async-done(((bf16[8,192,512]{2,1,0:T(8,128)(2,1)}), bf16[8,192,512]{2,1,0:T(8,128)(2,1)}, u32[]{:S(2)}, u32[]{:S(2)}) %all-to-all-start.6) | async-done | bytes 1572896 | tf_op jit(solution)/shard_map/all_to_all | solution.py:100
  330.3 3.5 %all-to-all-start.5 = ((bf16[4,128,384]{2,1,0:T(8,128)(2,1)}), bf16[4,128,384]{2,1,0:T(8,128)(2,1)S(1)}, u32[]{:S(2)}, u32[]{:S(2)}) async-start(bf16[4,128,384]{2,1,0:T(8,128)(2,1)} %copy.72), calls=%async_computation.5 | async-start | bytes 786432 | tf_op jit(solution)/shard_map/all_to_all | solution.py:39
  333.8 2.7 copy.80
  336.5 6.2 %all-to-all-done.5 = bf16[4,128,384]{2,1,0:T(8,128)(2,1)S(1)} async-done(((bf16[4,128,384]{2,1,0:T(8,128)(2,1)}), bf16[4,128,384]{2,1,0:T(8,128)(2,1)S(1)}, u32[]{:S(2)}, u32[]{:S(2)}) %all-to-all-start.5) | async-done | bytes 393248 | tf_op jit(solution)/shard_map/all_to_all | solution.py:39
  342.8 0.7 reduce_sum.65
  (20 shorter events, 0.1 us)
Async XLA Ops:
  0.6 138.7 %copy-start = (bf16[32,2,128,128]{3,2,1,0:T(8,128)(2,1)S(1)}, bf16[32,2,128,128]{3,2,1,0:T(8,128)(2,1)}, u32[]{:S(2)}) copy-start(bf16[32,2,128,128]{3,2,1,0:T(8,128)(2,1)} %param.10) | copy-start | bytes 6291460
  3.5 5.3 %copy-start.6 = (s32[128,2]{0,1:T(2,128)S(1)}, s32[128,2]{0,1:T(2,128)}, u32[]{:S(2)}) copy-start(s32[128,2]{0,1:T(2,128)} %param.9) | copy-start | bytes 3076
  3.5 26.4 %all-to-all-start.2 = ((bf16[192,8,512]{2,0,1:T(8,128)(2,1)}), bf16[192,8,512]{2,0,1:T(8,128)(2,1)}, u32[]{:S(2)}, u32[]{:S(2)}) async-start(bf16[192,8,512]{2,0,1:T(8,128)(2,1)} %bitcast.64), calls=%async_computation.2 | async-start | bytes 3145728 | tf_op jit(solution)/shard_map/all_to_all | solution.py:72
  26.3 100.4 %copy-start.5 = (bf16[128,1536]{1,0:T(8,128)(2,1)S(1)}, bf16[128,1536]{1,0:T(8,128)(2,1)}, u32[]{:S(2)}) copy-start(bf16[128,1536]{1,0:T(8,128)(2,1)} %param.6) | copy-start | bytes 1179652
  128.7 6.3 %copy-start.7 = (f32[128]{0:T(128)S(1)}, f32[128]{0:T(128)}, u32[]{:S(2)}) copy-start(f32[128]{0:T(128)} %param.11) | copy-start | bytes 1540
  128.7 42.9 %all-to-all-start.1 = ((bf16[8,128,1536]{2,1,0:T(8,128)(2,1)}), bf16[8,128,1536]{2,1,0:T(8,128)(2,1)}, u32[]{:S(2)}, u32[]{:S(2)}) async-start(bf16[8,128,1536]{2,1,0:T(8,128)(2,1)} %broadcast_in_dim.26), calls=%async_computation.1 | async-start | bytes 6291456 | tf_op jit(solution)/shard_map/all_to_all | solution.py:22
  171.6 92.5 %all-to-all-start.3 = ((bf16[128,8,512]{0,2,1:T(8,128)(2,1)}), bf16[128,8,512]{0,2,1:T(8,128)(2,1)S(1)}, u32[]{:S(2)}, u32[]{:S(2)}) async-start(bf16[128,8,512]{0,2,1:T(8,128)(2,1)} %bitcast.14), calls=%async_computation.3 | async-start | bytes 2097152 | tf_op jit(solution)/shard_map/all_to_all | solution.py:81
  221.8 2.2 copy-start.1
  266.3 3.7 %copy-start.3 = (bf16[1024,512]{0,1:T(8,128)(2,1)}, bf16[1024,512]{0,1:T(8,128)(2,1)S(1)}, u32[]{:S(2)}) copy-start(bf16[1024,512]{0,1:T(8,128)(2,1)S(1)} %fusion.3) | copy-start | bytes 3145732
  270.0 1.7 copy-start.2
  272.9 3.8 %collective-permute-start = (bf16[4,128,1536]{2,1,0:T(8,128)(2,1)}, bf16[4,128,1536]{2,1,0:T(8,128)(2,1)}, u32[]{:S(2)}, u32[]{:S(2)}) collective-permute-start(bf16[4,128,1536]{2,1,0:T(8,128)(2,1)} %dynamic-slice_bitcast_fusion), channel_id=1, source_target_pairs={{0,4},{4,0},{8,12},{12,8},{16,20},{20,16},{24,28},{28,24},{1,5},{5... | collective-permute-start | bytes 4718600 | tf_op jit(solution)/shard_map/ppermute | solution.py:33
  280.1 4.5 %copy-start.4 = (bf16[1024,512]{0,1:T(8,128)(2,1)S(1)}, bf16[1024,512]{0,1:T(8,128)(2,1)}, u32[]{:S(2)}) copy-start(bf16[1024,512]{0,1:T(8,128)(2,1)} %copy-done.3) | copy-start | bytes 3145732
  280.1 24.9 %all-to-all-start.4 = ((bf16[4,128,1536]{2,1,0:T(8,128)(2,1)}), bf16[4,128,1536]{2,1,0:T(8,128)(2,1)}, u32[]{:S(2)}, u32[]{:S(2)}) async-start(bf16[4,128,1536]{2,1,0:T(8,128)(2,1)} %fusion), calls=%async_computation.4 | async-start | bytes 3145728 | tf_op jit(solution)/shard_map/all_to_all | solution.py:36
  305.0 25.3 %all-to-all-start.6 = ((bf16[8,192,512]{2,1,0:T(8,128)(2,1)}), bf16[8,192,512]{2,1,0:T(8,128)(2,1)}, u32[]{:S(2)}, u32[]{:S(2)}) async-start(bf16[8,192,512]{2,1,0:T(8,128)(2,1)} %bitcast.65), calls=%async_computation.6 | async-start | bytes 3145728 | tf_op jit(solution)/shard_map/all_to_all | solution.py:100
  330.3 12.5 %all-to-all-start.5 = ((bf16[4,128,384]{2,1,0:T(8,128)(2,1)}), bf16[4,128,384]{2,1,0:T(8,128)(2,1)S(1)}, u32[]{:S(2)}, u32[]{:S(2)}) async-start(bf16[4,128,384]{2,1,0:T(8,128)(2,1)} %copy.72), calls=%async_computation.5 | async-start | bytes 786432 | tf_op jit(solution)/shard_map/all_to_all | solution.py:39
